TPU v7x, 32 devices: a whole 2x2x4 slice. The times are simulated.
32 devices in a mesh: cuts: 2 (over x), brick: 16 (over z, y, core).
Axes of the slice: x: 2, y: 2, z: 4, core: 2. Of those that a mesh axis runs over, the one named last changes fastest.
Arguments:
- eigen_vectors: float32 [64, 2, 3, 64, 512], P(None, None, None, ('cuts', 'brick')), parts along dimension 3, may hold values from -6 to 6
- link_field: float32 [3, 2, 3, 3, 64, 512], P(None, None, None, None, ('cuts', 'brick')), parts along dimension 4, may hold values from -3 to 3
- block_slot: int32 [63], replicated, may hold values from 0 to 63, as said below
Outputs:
- elementals: float32 [128, 32, 128], P(('cuts', 'brick')), parts along dimension 0
There are 2 independent parts, one for each index of `cuts`. A program takes and returns all parts, laid end to end along the dimension named above; an argument that names none is the same for every part. Nothing has to cross between parts.
Inputs may be any that keep to these rules, and one draw needn't show every extreme that they name: block_slot names distinct slots; slot s belongs to device s // 4 of the brick axis; in every draw some device has all 4 of its slots named.
All inputs are finite; a program needn't handle non-finite values.
Results may differ from a plain program's by a relative error of at most 0.0044.
Values sent between devices are 32-bit elements; how exact they have to be, the bound alone decides.
A program may use at most 64 MiB of HBM per device.

v0:
```python
import functools
import math

import jax
import jax.numpy as jnp
from jax import lax
from jax.experimental import pallas as pl
from jax.experimental.pallas import tpu as pltpu
from jax.sharding import PartitionSpec as P

PB = 32
CAP = 4
LX = 8
LY = 64


LANES = 128
VECTOR_GROUPS = 4
TILE = 8


def shifted_columns(row, column, forward):
    lanes = row.shape[-1]
    if forward:
        return jnp.where(
            column == LX - 1, pltpu.roll(row, LX - 1, 1), pltpu.roll(row, lanes - 1, 1)
        )
    return jnp.where(column == 0, pltpu.roll(row, lanes - LX + 1, 1), pltpu.roll(row, 1, 1))


def times_link(links, field, adjoint, totals):
    for row in range(3):
        for col in range(3):
            at = col * 3 + row if adjoint else row * 3 + col
            real, imag = links(at), links(9 + at)
            if adjoint:
                terms = (
                    real * field[col] + imag * field[3 + col],
                    real * field[3 + col] - imag * field[col],
                )
            else:
                terms = (
                    real * field[col] - imag * field[3 + col],
                    real * field[3 + col] + imag * field[col],
                )
            for part, term in zip((row, 3 + row), terms):
                totals[part] = term if totals[part] is None else totals[part] + term


def filter_kernel(
    eigen_ref,
    link_ref,
    out_ref,
    first_ref,
    near_halo,
    far_halo,
    lower_ref,
    wide_ref,
    send_sem,
    recv_sem,
    link_send,
    link_recv,
):
    planes, _, vectors, sites = eigen_ref.shape
    count = lax.axis_size("brick")
    me = lax.axis_index("brick")
    above = lax.rem(me + 1, count)
    below = lax.rem(me + count - 1, count)
    group_rows = vectors // VECTOR_GROUPS

    barrier = pltpu.get_barrier_semaphore()
    for other in (below, above):
        pl.semaphore_signal(
            barrier, inc=1, device_id={"brick": other}, device_id_type=pl.DeviceIdType.MESH
        )
    pl.semaphore_wait(barrier, 2)

    def halo_copy(hop, side, group):
        source = (eigen_ref, first_ref)[hop]
        target = (near_halo, far_halo)[hop]
        rows = pl.ds(group * group_rows, group_rows)
        return pltpu.make_async_remote_copy(
            src_ref=source.at[planes - 1 if side == 0 else 0, :, rows],
            dst_ref=target.at[side, :, rows],
            send_sem=send_sem.at[hop, side, group],
            recv_sem=recv_sem.at[hop, side, group],
            device_id={"brick": above if side == 0 else below},
            device_id_type=pl.DeviceIdType.MESH,
        )

    link_copy = pltpu.make_async_remote_copy(
        src_ref=link_ref.at[2, planes - 1],
        dst_ref=lower_ref,
        send_sem=link_send,
        recv_sem=link_recv,
        device_id={"brick": above},
        device_id_type=pl.DeviceIdType.MESH,
    )
    link_copy.start()
    for group in range(VECTOR_GROUPS):
        for side in range(2):
            halo_copy(0, side, group).start()

    def widen(direction, plane, block):
        for at in range(18):
            wide_ref[direction, at, plane] = jnp.broadcast_to(block[at : at + 1], (TILE, sites))

    link_column = lax.broadcasted_iota(jnp.int32, (18, sites), 1) % LX
    for plane in range(planes):
        along_x, along_y, along_z = (link_ref[axis, plane] for axis in range(3))
        widen(0, plane, along_x)
        widen(1, plane, shifted_columns(along_x, link_column, False))
        widen(2, plane, along_y)
        widen(3, plane, pltpu.roll(along_y, LX, 1))
        widen(4, plane, along_z)
        if plane > 0:
            widen(5, plane, link_ref[2, plane - 1])
    link_copy.wait_recv()
    widen(5, 0, lower_ref[...])

    lane = lax.broadcasted_iota(jnp.int32, (TILE, LANES), 1)
    column = lane % LX
    chunks = sites // LANES

    def hop_group(source, halo, group, plane, finish):
        def one_tile(at, carry):
            chunk = lax.rem(at, chunks)
            row = pl.multiple_of(group * group_rows + (at // chunks) * TILE, TILE)
            rows = pl.ds(row, TILE)

            def lanes_of(which):
                return pl.ds(pl.multiple_of(which * LANES, LANES), LANES)

            here = lanes_of(chunk)
            after = lanes_of(lax.rem(chunk + 1, chunks))
            before = lanes_of(lax.rem(chunk + chunks - 1, chunks))
            middle = [source[plane, part, rows, here] for part in range(6)]
            totals = [None] * 6

            def links(direction):
                return lambda at: wide_ref[direction, at, plane, :, here]

            field = [shifted_columns(cell, column, True) for cell in middle]
            times_link(links(0), field, False, totals)
            field = [shifted_columns(cell, column, False) for cell in middle]
            times_link(links(1), field, True, totals)
            field = [
                jnp.where(
                    lane < LANES - LX,
                    pltpu.roll(middle[part], LANES - LX, 1),
                    pltpu.roll(source[plane, part, rows, after], LANES - LX, 1),
                )
                for part in range(6)
            ]
            times_link(links(2), field, False, totals)
            field = [
                jnp.where(
                    lane >= LX,
                    pltpu.roll(middle[part], LX, 1),
                    pltpu.roll(source[plane, part, rows, before], LX, 1),
                )
                for part in range(6)
            ]
            times_link(links(3), field, True, totals)
            if plane + 1 < planes:
                field = [source[plane + 1, part, rows, here] for part in range(6)]
            else:
                field = [halo[1, part, rows, here] for part in range(6)]
            times_link(links(4), field, False, totals)
            if plane > 0:
                field = [source[plane - 1, part, rows, here] for part in range(6)]
            else:
                field = [halo[0, part, rows, here] for part in range(6)]
            times_link(links(5), field, True, totals)
            for part in range(6):
                finish(plane, part, rows, here, totals[part] * (1.0 / 6.0))
            return carry

        lax.fori_loop(0, chunks * (group_rows // TILE), one_tile, 0)

    def keep_first(plane, part, rows, here, value):
        first_ref[plane, part, rows, here] = value

    def keep_filtered(plane, part, rows, here, value):
        out_ref[plane, part, rows, here] = 2.0 * value - eigen_ref[plane, part, rows, here]

    for hop in range(2):
        for group in range(VECTOR_GROUPS):
            for side in range(2):
                halo_copy(hop, side, group).wait_recv()
            for plane in range(planes):
                if hop == 0:
                    hop_group(eigen_ref, near_halo, group, plane, keep_first)
                else:
                    hop_group(first_ref, far_halo, group, plane, keep_filtered)
            if hop == 0:
                for side in range(2):
                    halo_copy(1, side, group).start()
    link_copy.wait_send()
    for hop in range(2):
        for group in range(VECTOR_GROUPS):
            for side in range(2):
                halo_copy(hop, side, group).wait_send()


def filtered_field(eigen, links):
    planes, parts, vectors, sites = eigen.shape
    halo = pltpu.VMEM((2, parts, vectors, sites), jnp.float32)
    vmem = pl.BlockSpec(memory_space=pltpu.VMEM)
    copies = (2, 2, VECTOR_GROUPS)
    return pl.pallas_call(
        filter_kernel,
        in_specs=[vmem, vmem],
        out_specs=vmem,
        out_shape=jax.ShapeDtypeStruct(eigen.shape, jnp.float32),
        scratch_shapes=[
            pltpu.VMEM(eigen.shape, jnp.float32),
            halo,
            halo,
            pltpu.VMEM((18, sites), jnp.float32),
            pltpu.VMEM((6, 18, planes, TILE, sites), jnp.float32),
            pltpu.SemaphoreType.DMA(copies),
            pltpu.SemaphoreType.DMA(copies),
            pltpu.SemaphoreType.DMA,
            pltpu.SemaphoreType.DMA,
        ],
        compiler_params=pltpu.CompilerParams(
            collective_id=1, has_side_effects=True, vmem_limit_bytes=24 << 20
        ),
        name="filtered_field",
    )(eigen, links)


GROUP = 16
DOT_ROWS = 256


def pair_diquarks(left, right):
    parts = [None] * 6
    for colour in range(3):
        first = (colour + 1) % 3
        second = (colour + 2) % 3
        parts[colour] = (
            left[first] * right[second]
            - left[3 + first] * right[3 + second]
            - (left[second] * right[first] - left[3 + second] * right[3 + first])
        )
        parts[3 + colour] = (
            left[first] * right[3 + second]
            + left[3 + first] * right[second]
            - (left[second] * right[3 + first] + left[3 + second] * right[first])
        )
    return parts


def elemental_kernel(factor, slot_ref, field_ref, placed_ref, quark_ref, sum_ref, low_ref, pair_ref):
    vectors = field_ref.shape[1]
    step = pl.program_id(0)

    @pl.when(step == 0)
    def _():
        sum_ref[...] = jnp.zeros_like(sum_ref)

    for colour in range(3):
        real_low = field_ref[colour].astype(jnp.bfloat16)
        imag_low = field_ref[3 + colour].astype(jnp.bfloat16)
        real_at = slice(colour * LANES, (colour + 1) * LANES)
        imag_at = slice((3 + colour) * LANES, (4 + colour) * LANES)
        low_ref[:vectors, real_at] = real_low
        low_ref[:vectors, imag_at] = -imag_low
        low_ref[vectors:, real_at] = imag_low
        low_ref[vectors:, imag_at] = real_low

    base = 0
    row_starts = []
    for group in range(vectors // GROUP):
        width = vectors - group * GROUP
        row_starts += [base + at * width - group * GROUP for at in range(GROUP)]

        def one_left(at, carry, group=group, width=width, base=base):
            left = [
                jnp.broadcast_to(
                    field_ref[part, pl.ds(group * GROUP + at, 1), :], (GROUP, LANES)
                )
                for part in range(6)
            ]
            for tile in range(width // GROUP):
                from_row = (group + tile) * GROUP
                right = [field_ref[part, from_row : from_row + GROUP, :] for part in range(6)]
                parts = pair_diquarks(left, right)
                to_row = pl.multiple_of(base + at * width + tile * GROUP, GROUP)
                for part in range(6):
                    quark_ref[pl.ds(to_row, GROUP), part * LANES : (part + 1) * LANES] = parts[
                        part
                    ].astype(jnp.bfloat16)
            return carry

        lax.fori_loop(0, GROUP, one_left, 0)
        base += GROUP * width

    def one_dot(at, carry):
        rows = pl.ds(pl.multiple_of(at * DOT_ROWS, DOT_ROWS), DOT_ROWS)
        sum_ref[rows, :] += lax.dot_general(
            quark_ref[rows, :],
            low_ref[...],
            (((1,), (1,)), ((), ())),
            preferred_element_type=jnp.float32,
        )
        return carry

    lax.fori_loop(0, sum_ref.shape[0] // DOT_ROWS, one_dot, 0)

    @pl.when(step == pl.num_programs(0) - 1)
    def _():
        pair_at = 0
        for left in range(vectors - 1):
            count = vectors - 1 - left
            start = row_starts[left] + left + 1
            pair_ref[pair_at : pair_at + count, :] = sum_ref[start : start + count, :] * factor
            pair_at += count
        placed_ref[...] = jnp.zeros_like(placed_ref)

        def place(block, carry):
            rows = pl.ds(pl.multiple_of(block * PB, PB), PB)
            placed_ref[slot_ref[block]] = pair_ref[rows, :]
            return carry

        lax.fori_loop(0, slot_ref.shape[0], place, 0)


def elemental_sums(field, block_slot, factor, slot_total):
    planes, _, vectors, sites = field.shape
    chunks = sites // LANES
    groups = vectors // GROUP
    rows = GROUP * GROUP * (groups * (groups + 1) // 2)
    pairs = block_slot.shape[0] * PB
    return pl.pallas_call(
        functools.partial(elemental_kernel, factor),
        grid=(planes * chunks,),
        in_specs=[
            pl.BlockSpec(memory_space=pltpu.SMEM),
            pl.BlockSpec(
                (None, 6, vectors, LANES), lambda at: (at // chunks, 0, 0, at % chunks)
            ),
        ],
        out_specs=pl.BlockSpec((slot_total, PB, 2 * vectors), lambda at: (0, 0, 0)),
        out_shape=jax.ShapeDtypeStruct((slot_total, PB, 2 * vectors), jnp.float32),
        scratch_shapes=[
            pltpu.VMEM((rows, 6 * LANES), jnp.bfloat16),
            pltpu.VMEM((rows, 2 * vectors), jnp.float32),
            pltpu.VMEM((2 * vectors, 6 * LANES), jnp.bfloat16),
            pltpu.VMEM((pairs, 2 * vectors), jnp.float32),
        ],
        compiler_params=pltpu.CompilerParams(vmem_limit_bytes=40 << 20),
        name="elemental_sums",
    )(block_slot, field)


PIECES = 4


def scatter_kernel(levels, placed_ref, out_ref, *scratch):
    held = (placed_ref,) + scratch[: levels - 1]
    landed = scratch[levels - 1 : 2 * levels - 1]
    send_sem, recv_sem = scratch[2 * levels - 1 :]
    me = lax.axis_index("brick")
    bits = [lax.rem(me // (1 << level), 2) for level in range(levels)]
    partners = [me + (1 - 2 * bits[level]) * (1 << level) for level in range(levels)]

    barrier = pltpu.get_barrier_semaphore()
    for partner in partners:
        pl.semaphore_signal(
            barrier, inc=1, device_id={"brick": partner}, device_id_type=pl.DeviceIdType.MESH
        )
    pl.semaphore_wait(barrier, levels)

    rows = out_ref.shape[0] // PIECES

    def view(level, piece, bit):
        whole = (slice(None),) * (levels - level - 1)
        return whole + (bit, pl.ds(piece * rows, rows))

    def copy(level, piece):
        whole = (slice(None),) * (levels - level - 1)
        return pltpu.make_async_remote_copy(
            src_ref=held[level].at[view(level, piece, 1 - bits[level])],
            dst_ref=landed[level].at[whole + (pl.ds(piece * rows, rows),)],
            send_sem=send_sem.at[level, piece],
            recv_sem=recv_sem.at[level, piece],
            device_id={"brick": partners[level]},
            device_id_type=pl.DeviceIdType.MESH,
        )

    for piece in range(PIECES):
        copy(0, piece).start()
    for level in range(levels):
        for piece in range(PIECES):
            copy(level, piece).wait_recv()
            whole = (slice(None),) * (levels - level - 1)
            part = whole + (pl.ds(piece * rows, rows),)
            total = held[level][view(level, piece, bits[level])] + landed[level][part]
            if level + 1 < levels:
                held[level + 1][part] = total
                copy(level + 1, piece).start()
            else:
                out_ref[part] = total
    for level in range(levels):
        for piece in range(PIECES):
            copy(level, piece).wait_send()


def scatter_sums(placed):
    devices = lax.axis_size("brick")
    levels = devices.bit_length() - 1
    rows = placed.shape[0] // devices * placed.shape[1]
    width = placed.shape[2]
    shapes = [(2,) * (levels - level) + (rows, width) for level in range(levels + 1)]
    out = pl.pallas_call(
        functools.partial(scatter_kernel, levels),
        in_specs=[pl.BlockSpec(memory_space=pltpu.VMEM)],
        out_specs=pl.BlockSpec(memory_space=pltpu.VMEM),
        out_shape=jax.ShapeDtypeStruct((rows, width), jnp.float32),
        scratch_shapes=[pltpu.VMEM(shape, jnp.float32) for shape in shapes[1:levels]]
        + [pltpu.VMEM(shape, jnp.float32) for shape in shapes[1:]]
        + [pltpu.SemaphoreType.DMA((levels, PIECES)), pltpu.SemaphoreType.DMA((levels, PIECES))],
        compiler_params=pltpu.CompilerParams(
            collective_id=0, has_side_effects=True, vmem_limit_bytes=24 << 20
        ),
        name="scatter_sums",
    )(placed.reshape(shapes[0]))
    return out.reshape(placed.shape[0] // devices, placed.shape[1], width)


def on_device(eigen_vectors, link_field, block_slot):
    vector_count = eigen_vectors.shape[0]
    planes, sites = eigen_vectors.shape[3:]
    eigen = jnp.transpose(eigen_vectors, (3, 1, 2, 0, 4)).reshape(planes, 6, vector_count, sites)
    links = jnp.transpose(link_field, (0, 4, 1, 2, 3, 5)).reshape(3, planes, 18, sites)
    brick_count = lax.axis_size("brick")
    factor = 1.0 / math.sqrt(3.0 * LX * LY * planes * brick_count)
    field = filtered_field(eigen, links)
    return scatter_sums(elemental_sums(field, block_slot, factor, CAP * brick_count))


def solution(mesh):
    return jax.shard_map(
        on_device,
        mesh=mesh,
        in_specs=(
            P(None, None, None, ("cuts", "brick"), None),
            P(None, None, None, None, ("cuts", "brick"), None),
            P(),
        ),
        out_specs=P(("cuts", "brick"), None, None),
        check_vma=False,
    )
```

profile of v0, /device:TPU:0, one launch (start us, length us, event | category | flops | bytes accessed | tf_op | source)
XLA Modules:
  0.0 106.7 jit_solution(17140575293994574149)
XLA Ops:
  0.0 1.0 copy.7.link_ref
  1.0 1.9 %copy.6 = f32[2,2,3,64,512]{4,3,2,1,0:T(8,128)S(1)} copy(f32[2,2,3,64,512]{4,0,2,1,3:T(2,128)} %bitcast.10) | data formatting | bytes 3145728 | tf_op jit(solution)/shard_map/transpose | solution.py:437
  2.9 0.0 copy-start
  2.9 36.3 %filtered_field.1.field_ref = f32[2,6,64,512]{3,2,1,0:T(8,128)S(1)} custom-call(f32[2,6,64,512]{3,2,1,0:T(8,128)S(1)} %bitcast.7, f32[3,2,18,512]{3,2,1,0:T(8,128)S(1)} %copy.7.link_ref), custom_call_target="tpu_custom_call" | custom-call | tf_op jit(solution)/shard_map/filtered_field/pallas_call | solution.py:211
  39.3 0.0 copy-done
  39.3 42.5 %elemental_sums.1 = f32[64,32,128]{2,1,0:T(8,128)S(1)} custom-call(s32[63]{0:T(128)S(1)} %copy-done, f32[2,6,64,512]{3,2,1,0:T(8,128)S(1)} %filtered_field.1.field_ref), custom_call_target="tpu_custom_call" | custom-call | tf_op jit(solution)/shard_map/elemental_sums/pallas_call | solution.py:337
  81.8 24.2 %scatter_sums.1 = f32[128,128]{1,0:T(8,128)S(1)} custom-call(f32[2,2,2,2,128,128]{5,4,3,2,1,0:T(8,128)S(1)} %bitcast.8), custom_call_target="tpu_custom_call" | custom-call | tf_op jit(solution)/shard_map/scatter_sums/pallas_call | solution.py:418
  106.0 0.6 copy.9
Async XLA Ops:
  2.9 36.4 %copy-start = (s32[63]{0:T(128)S(1)}, s32[63]{0:T(128)}, u32[]{:S(2)}) copy-start(s32[63]{0:T(128)} %slot_ref.1) | copy-start | bytes 760
where the time goes:
time: 107 us
  Pallas kernels  103 us (96%)
  local copies, waits for them, and re-layouts  3.54 us (3%)
    pallas_call x1, Pallas kernels, elemental_sums(): pl.pallas_call(functools.partial(elemental_kernel, factor), grid=(planes...  42.5 us
    pallas_call x1, Pallas kernels, filtered_field(): pl.pallas_call(filter_kernel, in_specs=[vmem, vmem], out_specs=vmem, out_...  36.3 us
    pallas_call x1, Pallas kernels, scatter_sums(): pl.pallas_call(functools.partial(scatter_kernel, levels), in_specs=[pl.Bl...  24.2 us

commit v1 on v0

--- a/solution.py
+++ b/solution.py
@@ -231,8 +231,8 @@
     )(eigen, links)
 
 
-GROUP = 16
-DOT_ROWS = 256
+ROW_TILE = 8
+DOT_TILES = 40
 
 
 def pair_diquarks(left, right):
@@ -240,20 +240,27 @@
     for colour in range(3):
         first = (colour + 1) % 3
         second = (colour + 2) % 3
-        parts[colour] = (
-            left[first] * right[second]
-            - left[3 + first] * right[3 + second]
-            - (left[second] * right[first] - left[3 + second] * right[3 + first])
-        )
-        parts[3 + colour] = (
-            left[first] * right[3 + second]
-            + left[3 + first] * right[second]
-            - (left[second] * right[3 + first] + left[3 + second] * right[first])
-        )
+        common = left[6 + first] * right[second] - left[6 + second] * right[first]
+        turned = left[first] * right[3 + second] - left[second] * right[3 + first]
+        summed = left[3 + first] * right[6 + second] - left[3 + second] * right[6 + first]
+        parts[colour] = common - summed
+        parts[3 + colour] = common + turned
     return parts
 
 
-def elemental_kernel(factor, slot_ref, field_ref, placed_ref, quark_ref, sum_ref, low_ref, pair_ref):
+def row_tiles(vectors):
+    tiles = []
+    row_starts = []
+    for left in range(vectors - 1):
+        lowest = (left + 1) // ROW_TILE
+        row_starts.append((len(tiles) - lowest) * ROW_TILE)
+        tiles += [(left, tile) for tile in range(lowest, vectors // ROW_TILE)]
+    return tiles, row_starts
+
+
+def elemental_kernel(
+    factor, slot_ref, field_ref, placed_ref, quark_ref, sum_ref, low_ref, pair_ref, mixed_ref
+):
     vectors = field_ref.shape[1]
     step = pl.program_id(0)
 
@@ -262,8 +269,12 @@
         sum_ref[...] = jnp.zeros_like(sum_ref)
 
     for colour in range(3):
-        real_low = field_ref[colour].astype(jnp.bfloat16)
-        imag_low = field_ref[3 + colour].astype(jnp.bfloat16)
+        real = field_ref[colour]
+        imag = field_ref[3 + colour]
+        mixed_ref[colour] = imag - real
+        mixed_ref[3 + colour] = imag + real
+        real_low = real.astype(jnp.bfloat16)
+        imag_low = imag.astype(jnp.bfloat16)
         real_at = slice(colour * LANES, (colour + 1) * LANES)
         imag_at = slice((3 + colour) * LANES, (4 + colour) * LANES)
         low_ref[:vectors, real_at] = real_low
@@ -271,44 +282,36 @@
         low_ref[vectors:, real_at] = imag_low
         low_ref[vectors:, imag_at] = real_low
 
-    base = 0
-    row_starts = []
-    for group in range(vectors // GROUP):
-        width = vectors - group * GROUP
-        row_starts += [base + at * width - group * GROUP for at in range(GROUP)]
-
-        def one_left(at, carry, group=group, width=width, base=base):
-            left = [
-                jnp.broadcast_to(
-                    field_ref[part, pl.ds(group * GROUP + at, 1), :], (GROUP, LANES)
-                )
-                for part in range(6)
-            ]
-            for tile in range(width // GROUP):
-                from_row = (group + tile) * GROUP
-                right = [field_ref[part, from_row : from_row + GROUP, :] for part in range(6)]
-                parts = pair_diquarks(left, right)
-                to_row = pl.multiple_of(base + at * width + tile * GROUP, GROUP)
-                for part in range(6):
-                    quark_ref[pl.ds(to_row, GROUP), part * LANES : (part + 1) * LANES] = parts[
-                        part
-                    ].astype(jnp.bfloat16)
-            return carry
-
-        lax.fori_loop(0, GROUP, one_left, 0)
-        base += GROUP * width
-
-    def one_dot(at, carry):
-        rows = pl.ds(pl.multiple_of(at * DOT_ROWS, DOT_ROWS), DOT_ROWS)
+    tiles, row_starts = row_tiles(vectors)
+
+    def one_tile(left_at, tile):
+        rows = slice(tile * ROW_TILE, (tile + 1) * ROW_TILE)
+
+        def spread(ref, part):
+            return jnp.broadcast_to(ref[part, left_at : left_at + 1, :], (ROW_TILE, LANES))
+
+        left = [spread(field_ref, part) for part in range(6)]
+        left += [spread(mixed_ref, 3 + colour) for colour in range(3)]
+        right = [field_ref[colour, rows, :] for colour in range(3)]
+        right += [mixed_ref[part, rows, :] for part in range(6)]
+        return pair_diquarks(left, right)
+
+    for from_tile in range(0, len(tiles), DOT_TILES):
+        to_tile = min(from_tile + DOT_TILES, len(tiles))
+        for at in range(from_tile, to_tile, 2):
+            upper = one_tile(*tiles[at])
+            lower = one_tile(*tiles[at + 1])
+            for part in range(6):
+                quark_ref[
+                    at * ROW_TILE : (at + 2) * ROW_TILE, part * LANES : (part + 1) * LANES
+                ] = jnp.concatenate([upper[part], lower[part]], 0).astype(jnp.bfloat16)
+        rows = slice(from_tile * ROW_TILE, to_tile * ROW_TILE)
         sum_ref[rows, :] += lax.dot_general(
             quark_ref[rows, :],
             low_ref[...],
             (((1,), (1,)), ((), ())),
             preferred_element_type=jnp.float32,
         )
-        return carry
-
-    lax.fori_loop(0, sum_ref.shape[0] // DOT_ROWS, one_dot, 0)
 
     @pl.when(step == pl.num_programs(0) - 1)
     def _():
@@ -331,8 +334,7 @@
 def elemental_sums(field, block_slot, factor, slot_total):
     planes, _, vectors, sites = field.shape
     chunks = sites // LANES
-    groups = vectors // GROUP
-    rows = GROUP * GROUP * (groups * (groups + 1) // 2)
+    rows = len(row_tiles(vectors)[0]) * ROW_TILE
     pairs = block_slot.shape[0] * PB
     return pl.pallas_call(
         functools.partial(elemental_kernel, factor),
@@ -350,6 +352,7 @@
             pltpu.VMEM((rows, 2 * vectors), jnp.float32),
             pltpu.VMEM((2 * vectors, 6 * LANES), jnp.bfloat16),
             pltpu.VMEM((pairs, 2 * vectors), jnp.float32),
+            pltpu.VMEM((6, vectors, LANES), jnp.float32),
         ],
         compiler_params=pltpu.CompilerParams(vmem_limit_bytes=40 << 20),
         name="elemental_sums",

time: 107 us -> 81.5 us (0.76)
  Pallas kernels: 103 us -> 77.8 us
    pallas_call x1, Pallas kernels: 42.5 us -> 17.3 us  [elemental_sums(): pl.pallas_call(functools.partial(elemental_kernel, factor), grid=(planes...]
where the time goes in v1:
time: 81.5 us; the launch traced here: 81.4 us
  Pallas kernels  77.8 us (95%)
  local copies, waits for them, and re-layouts  3.54 us (4%)
    pallas_call x1, Pallas kernels, filtered_field(): pl.pallas_call(filter_kernel, in_specs=[vmem, vmem], out_specs=vmem, out_...  36.3 us
    pallas_call x1, Pallas kernels, scatter_sums(): pl.pallas_call(functools.partial(scatter_kernel, levels), in_specs=[pl.Bl...  24.1 us
    pallas_call x1, Pallas kernels, elemental_sums(): pl.pallas_call(functools.partial(elemental_kernel, factor), grid=(planes...  17.3 us
    transpose x1, local copies, waits for them, and re-layouts, on_device(): jnp.transpose(eigen_vectors, (3, 1, 2, 0, 4))  1.92 us

profile of v1, /device:TPU:0, one launch (start us, length us, event | category | flops | bytes accessed | tf_op | source)
XLA Modules:
  0.0 81.4 jit_solution(15216555480121046980)
XLA Ops:
  0.0 1.0 %copy.7.link_ref = f32[3,2,18,512]{3,2,1,0:T(8,128)S(1)} copy(f32[3,2,18,512]{3,1,2,0:T(2,128)} %bitcast.11) | data formatting | bytes 442368 | tf_op jit(solution)/shard_map/reshape | solution.py:441
  1.0 1.9 %copy.6 = f32[2,2,3,64,512]{4,3,2,1,0:T(8,128)S(1)} copy(f32[2,2,3,64,512]{4,0,2,1,3:T(2,128)} %bitcast.10) | data formatting | bytes 3145728 | tf_op jit(solution)/shard_map/transpose | solution.py:440
  2.9 0.0 copy-start
  2.9 36.3 %filtered_field.1.field_ref = f32[2,6,64,512]{3,2,1,0:T(8,128)S(1)} custom-call(f32[2,6,64,512]{3,2,1,0:T(8,128)S(1)} %bitcast.7, f32[3,2,18,512]{3,2,1,0:T(8,128)S(1)} %copy.7.link_ref), custom_call_target="tpu_custom_call" | custom-call | tf_op jit(solution)/shard_map/filtered_field/pallas_call | solution.py:211
  39.3 0.0 copy-done
  39.3 17.3 %elemental_sums.1 = f32[64,32,128]{2,1,0:T(8,128)S(1)} custom-call(s32[63]{0:T(128)S(1)} %copy-done, f32[2,6,64,512]{3,2,1,0:T(8,128)S(1)} %filtered_field.1.field_ref), custom_call_target="tpu_custom_call" | custom-call | tf_op jit(solution)/shard_map/elemental_sums/pallas_call | solution.py:339
  56.6 24.1 %scatter_sums.1 = f32[128,128]{1,0:T(8,128)S(1)} custom-call(f32[2,2,2,2,128,128]{5,4,3,2,1,0:T(8,128)S(1)} %bitcast.8), custom_call_target="tpu_custom_call" | custom-call | tf_op jit(solution)/shard_map/scatter_sums/pallas_call | solution.py:421
  80.7 0.6 copy.9
Async XLA Ops:
  2.9 36.4 %copy-start = (s32[63]{0:T(128)S(1)}, s32[63]{0:T(128)}, u32[]{:S(2)}) copy-start(s32[63]{0:T(128)} %slot_ref.1) | copy-start | bytes 760

commit v2 on v1

--- a/solution.py
+++ b/solution.py
@@ -15,7 +15,7 @@
 
 
 LANES = 128
-VECTOR_GROUPS = 4
+VECTOR_GROUPS = 8
 TILE = 8
 
 
@@ -359,7 +359,7 @@
     )(block_slot, field)
 
 
-PIECES = 4
+PIECES = 8
 
 
 def scatter_kernel(levels, placed_ref, out_ref, *scratch):

time: 81.5 us -> 80.9 us (level)
    pallas_call x1, Pallas kernels: 36.3 us -> 34.3 us  [filtered_field(): pl.pallas_call(filter_kernel, in_specs=[vmem, vmem], out_specs=vmem, out_...]
    pallas_call x1, Pallas kernels: 24.1 us -> 25.5 us  [scatter_sums(): pl.pallas_call(functools.partial(scatter_kernel, levels), in_specs=[pl.Bl...]
where the time goes in v2:
time: 80.9 us; the launch traced here: 80.7 us
  Pallas kernels  77.1 us (95%)
  local copies, waits for them, and re-layouts  3.54 us (4%)
    pallas_call x1, Pallas kernels, filtered_field(): pl.pallas_call(filter_kernel, in_specs=[vmem, vmem], out_specs=vmem, out_...  34.3 us
    pallas_call x1, Pallas kernels, scatter_sums(): pl.pallas_call(functools.partial(scatter_kernel, levels), in_specs=[pl.Bl...  25.5 us
    pallas_call x1, Pallas kernels, elemental_sums(): pl.pallas_call(functools.partial(elemental_kernel, factor), grid=(planes...  17.3 us
    transpose x1, local copies, waits for them, and re-layouts, on_device(): jnp.transpose(eigen_vectors, (3, 1, 2, 0, 4))  1.92 us

profile of v2, /device:TPU:0, one launch (start us, length us, event | category | flops | bytes accessed | tf_op | source)
XLA Modules:
  0.0 80.7 jit_solution(14101940666581066723)
XLA Ops:
  0.0 1.0 %copy.7.link_ref = f32[3,2,18,512]{3,2,1,0:T(8,128)S(1)} copy(f32[3,2,18,512]{3,1,2,0:T(2,128)} %bitcast.11) | data formatting | bytes 442368 | tf_op jit(solution)/shard_map/reshape | solution.py:441
  1.0 1.9 %copy.6 = f32[2,2,3,64,512]{4,3,2,1,0:T(8,128)S(1)} copy(f32[2,2,3,64,512]{4,0,2,1,3:T(2,128)} %bitcast.10) | data formatting | bytes 3145728 | tf_op jit(solution)/shard_map/transpose | solution.py:440
  2.9 0.0 copy-start
  2.9 34.3 %filtered_field.1.field_ref = f32[2,6,64,512]{3,2,1,0:T(8,128)S(1)} custom-call(f32[2,6,64,512]{3,2,1,0:T(8,128)S(1)} %bitcast.7, f32[3,2,18,512]{3,2,1,0:T(8,128)S(1)} %copy.7.link_ref), custom_call_target="tpu_custom_call" | custom-call | tf_op jit(solution)/shard_map/filtered_field/pallas_call | solution.py:211
  37.3 0.0 copy-done
  37.3 17.3 %elemental_sums.1 = f32[64,32,128]{2,1,0:T(8,128)S(1)} custom-call(s32[63]{0:T(128)S(1)} %copy-done, f32[2,6,64,512]{3,2,1,0:T(8,128)S(1)} %filtered_field.1.field_ref), custom_call_target="tpu_custom_call" | custom-call | tf_op jit(solution)/shard_map/elemental_sums/pallas_call | solution.py:339
  54.6 25.5 %scatter_sums.1 = f32[128,128]{1,0:T(8,128)S(1)} custom-call(f32[2,2,2,2,128,128]{5,4,3,2,1,0:T(8,128)S(1)} %bitcast.8), custom_call_target="tpu_custom_call" | custom-call | tf_op jit(solution)/shard_map/scatter_sums/pallas_call | solution.py:421
  80.1 0.6 copy.9
Async XLA Ops:
  2.9 34.4 %copy-start = (s32[63]{0:T(128)S(1)}, s32[63]{0:T(128)}, u32[]{:S(2)}) copy-start(s32[63]{0:T(128)} %slot_ref.1) | copy-start | bytes 760
